TPU v7x, 32 devices: a whole 2x2x4 slice. The times are simulated.
32 devices in a mesh: loop: 4 (over y, core), inner: 8 (over z, x).
Axes of the slice: x: 2, y: 2, z: 4, core: 2. Of those that a mesh axis runs over, the one named last changes fastest.
Arguments:
- snapshots: bfloat16 [8192, 1024], P(('loop', 'inner')), may hold values from -6 to 6
- bins: int32 [8192], replicated, may hold values from 0 to 63, as said below
- pairs: int32 [256, 2], replicated, may hold values from 0 to 63, as said below
- start_weights: bfloat16 [1024, 32], replicated, may hold values from -0.1875 to 0.1875
Outputs:
- basis: float32 [8192, 96], P(('loop', 'inner'))
- coefficients: float32 [4, 32, 32], replicated
Inputs may be any that keep to these rules, and one draw needn't show every extreme that they name: `bins`: the snapshot in row n has a bin in [r * 8, (r + 1) * 8), where r = (n // 256) mod (8). `pairs`: every row (a, b) has a <= b <= a + 8; every bin is paired with itself.
All inputs are finite; a program needn't handle non-finite values.
Results may differ from a plain program's by a relative error of at most 0.0003.
Values may be sent and summed in bfloat16 or wider, within the bound.
No kernel may reach another device: no remote copies, remote signals or barrier semaphores. Data moves between devices by JAX's collectives and lax.ppermute only.
A program may use at most 64 MiB of HBM per device.

v0:
```python
import jax
import jax.numpy as jnp
from jax import lax
from jax.sharding import PartitionSpec as P

STEPS = 2
BINS_COL = 8


def extended(cells, sides, width):
    for axis, dim in sides:
        count = lax.axis_size(axis)
        ends = count - 1
        head = lax.slice_in_dim(cells, 0, width, axis=dim)
        tail = lax.slice_in_dim(cells, cells.shape[dim] - width, cells.shape[dim], axis=dim)
        cells = jnp.concatenate(
            [
                lax.ppermute(tail, axis, [(i, (i + 1) % count) for i in range(ends)]),
                cells,
                lax.ppermute(head, axis, [((i + 1) % count, i) for i in range(ends)]),
            ],
            axis=dim,
        )
    return cells


def matches(values, targets):
    return (values[:, None] == targets[None, :]).astype(jnp.float32)


def local_gram(left, right):
    return jnp.dot(left.T, right, precision=lax.Precision.HIGHEST)


def finish(matrix, gram_total):
    lower_factor = jnp.linalg.cholesky(gram_total)
    result = lax.linalg.triangular_solve(
        lower_factor, matrix, left_side=False, lower=True, transpose_a=True
    )
    return (result, lower_factor.T)


def local(snapshots, bins, pairs, start_weights):
    row_count, features = snapshots.shape
    block_width = start_weights.shape[1]
    n_loop = lax.axis_size("loop")
    n_inner = lax.axis_size("inner")
    column = lax.axis_index("inner")
    group = lax.axis_index("loop")
    bin_grid = jnp.pad(
        bins.reshape(n_loop, n_inner, row_count), ((0, 0), (1, 1), (0, 0)), constant_values=-1
    )
    side_rows = extended(snapshots, (("inner", 0),), row_count)
    partner_rows = lax.all_gather(side_rows[None], "loop", axis=0, tiled=True)
    tile_rows = partner_rows.reshape(n_loop * 3 * row_count, features)
    tile_bins = lax.dynamic_slice_in_dim(bin_grid, column, 3, 1).reshape(-1)
    my_bins = lax.dynamic_slice_in_dim(bins, (group * n_inner + column) * row_count, row_count)
    bin_base = column * BINS_COL
    my_ids = bin_base + jnp.arange(BINS_COL, dtype=jnp.int32)
    window_ids = bin_base - BINS_COL + jnp.arange(3 * BINS_COL, dtype=jnp.int32)
    left_bins = pairs[:, 0]
    right_bins = pairs[:, 1]
    pair_count = jnp.dot(
        matches(left_bins, my_ids).T,
        matches(right_bins, window_ids),
        precision=lax.Precision.HIGHEST,
    )
    pair_count = pair_count + jnp.dot(
        matches(right_bins, my_ids).T,
        matches(left_bins, window_ids),
        precision=lax.Precision.HIGHEST,
    )
    linked_bins = jnp.where(pair_count > 0.5, 1.0, 0.0).astype(jnp.float32)
    my_hot = matches(my_bins, my_ids)
    row_links = jnp.dot(my_hot, linked_bins)
    mine_wide = snapshots.astype(jnp.float32)
    mine_norms = jnp.sum(mine_wide * mine_wide, axis=1)
    epsilon = features / 3.0
    part_hot = matches(tile_bins, window_ids) * (tile_bins >= 0).astype(jnp.float32)[:, None]
    band_mask = jnp.dot(row_links, part_hot.T)
    part_wide = tile_rows.astype(jnp.float32)
    part_norms = jnp.sum(part_wide * part_wide, axis=1)
    products = lax.dot_general(
        snapshots, tile_rows, (((1,), (1,)), ((), ())), preferred_element_type=jnp.float32
    )
    distance = mine_norms[:, None] + part_norms[None, :] - 2.0 * products
    kept_tiles = [band_mask * jnp.exp(-distance / epsilon)]

    def current_kernel(which):
        return kept_tiles[which]

    degree = jnp.sum(current_kernel(0), axis=1)
    inv_root = lax.rsqrt(degree)
    start_block = jnp.dot(snapshots, start_weights, preferred_element_type=jnp.float32)
    start_total = lax.psum(local_gram(start_block, start_block), ("loop", "inner"))
    current, unused = finish(start_block, start_total)
    basis_blocks = [current]
    coefficients = []
    previous = current
    prev_b = jnp.zeros((block_width, block_width), jnp.float32)
    for lanczos_step in range(STEPS):
        scaled = inv_root[:, None] * current
        vec_side = extended(scaled, (("inner", 0),), row_count)
        vec_strip = lax.all_gather(vec_side[None], "loop", axis=0, tiled=True)
        strip = vec_strip.reshape(n_loop * 3 * row_count, block_width)
        total = jnp.dot(current_kernel(0), strip, precision=lax.Precision.HIGHEST)
        image = inv_root[:, None] * total
        projected = lax.psum(local_gram(current, image), ("loop", "inner"))
        image = image - jnp.dot(current, projected, precision=lax.Precision.HIGHEST)
        if lanczos_step > 0:
            image = image - jnp.dot(previous, prev_b.T, precision=lax.Precision.HIGHEST)
        gram_total = lax.psum(local_gram(image, image), ("loop", "inner"))
        following, factor = finish(image, gram_total)
        coefficients.append(projected)
        coefficients.append(factor)
        previous = current
        prev_b = factor
        current = following
        basis_blocks.append(current)
    return (jnp.concatenate(basis_blocks, axis=1), jnp.stack(coefficients))


def solution(mesh):
    in_specs = (P(("loop", "inner"), None), P(), P(), P())
    out_specs = (P(("loop", "inner"), None), P())
    return jax.shard_map(local, mesh=mesh, in_specs=in_specs, out_specs=out_specs, check_vma=False)
```

profile of v0, /device:TPU:0, one launch (start us, length us, event | category | flops | bytes accessed | tf_op | source)
XLA Modules:
  0.0 321.3 jit_solution(17234646396150438926)
XLA Ops:
  8.7 5.5 %collective-permute-start = (bf16[256,1024]{1,0:T(8,128)(2,1)}, bf16[256,1024]{1,0:T(8,128)(2,1)S(1)}, u32[]{:S(2)}, u32[]{:S(2)}) collective-permute-start(bf16[256,1024]{1,0:T(8,128)(2,1)} %param.7), channel_id=1, source_target_pairs={{0,1},{1,2},{2,3},{3,4},{4,5},{5,6},{6,7},{8,9},{9,10},{10,11},{11... | collective-permute-start | bytes 1572872 | tf_op jit(solution)/shard_map/ppermute | solution.py:18
  14.2 10.2 %collective-permute-done.1 = bf16[256,1024]{1,0:T(8,128)(2,1)S(1)} collective-permute-done((bf16[256,1024]{1,0:T(8,128)(2,1)}, bf16[256,1024]{1,0:T(8,128)(2,1)S(1)}, u32[]{:S(2)}, u32[]{:S(2)}) %collective-permute-start.1) | collective-permute-done | bytes 524320 | tf_op jit(solution)/shard_map/ppermute | solution.py:20
  24.4 11.5 %collective-permute-done = bf16[256,1024]{1,0:T(8,128)(2,1)S(1)} collective-permute-done((bf16[256,1024]{1,0:T(8,128)(2,1)}, bf16[256,1024]{1,0:T(8,128)(2,1)S(1)}, u32[]{:S(2)}, u32[]{:S(2)}) %collective-permute-start) | collective-permute-done | bytes 524320 | tf_op jit(solution)/shard_map/ppermute | solution.py:18
  35.9 2.3 pad_maximum_fusion
  38.8 42.3 %psum.35 = f32[32,32]{0,1:T(8,128)S(1)} all-reduce(f32[32,32]{0,1:T(8,128)S(1)} %fusion.56), channel_id=1, replica_groups=mesh['loop'=4,'inner'=8] {'loop','inner'}, use_global_device_ids=true, to_apply=%region_0.1 | all-reduce | flops 1024 | bytes 8192 | tf_op jit(solution)/shard_map/psum | solution.py:95
  81.2 2.9 cholesky.59
  85.4 2.4 custom-call.7
  88.7 4.2 %multiply_reduce_fusion = f32[3072]{0:T(1024)S(1)} fusion(bf16[3072,1024]{1,0:T(8,128)(2,1)} %all-gather.5.cloned.1.call-done), kind=kLoop, calls=%fused_computation | loop fusion | flops 9434112 | bytes 6303744 | tf_op jit(solution)/shard_map/reduce_sum | solution.py:82
  93.3 4.0 %fusion.4 = f32[256,3072]{1,0:T(8,128)} fusion(bf16[3072,1024]{1,0:T(8,128)(2,1)S(1)} %copy-done.1, bf16[256,1024]{1,0:T(8,128)(2,1)S(1)} %copy-done.2, f32[3072]{0:T(1024)S(1)} %multiply_reduce_fusion, f32[256]{0:T(256)S(1)} %multiply_reduce_fusion.1), kind=kOutput, calls=%fused_computation.7 | convolution fusion | flops 1614544896 | bytes 9974784 | tf_op jit(solution)/shard_map/dot_general | solution.py:83
  97.3 2.8 fusion.52
  101.6 4.8 %collective-permute-start.2 = (f32[256,32]{0,1:T(8,128)S(1)}, f32[256,32]{0,1:T(8,128)S(1)}, u32[]{:S(2)}, u32[]{:S(2)}) collective-permute-start(f32[256,32]{0,1:T(8,128)S(1)} %get-tuple-element.18), channel_id=1, source_target_pairs={{0,1},{1,2},{2,3},{3,4},{4,5},{5,6},{6,7},{8,9},{9,10},{10,11},{11... | collective-permute-start | bytes 98312 | tf_op jit(solution)/shard_map/ppermute | solution.py:18
  108.0 7.2 %all-gather.1 = f32[3072,32]{0,1:T(8,128)S(1)} all-gather(f32[768,32]{0,1:T(8,128)S(1)} %pad_maximum_fusion.1), channel_id=3, replica_groups=mesh['loop'=4,'inner'=8] {'loop'}, dimensions={0}, use_global_device_ids=true | all-gather | bytes 491520 | tf_op jit(solution)/shard_map/all_gather | solution.py:104
  115.2 2.8 convolution_multiply_fusion.3
  118.1 41.4 %psum.36 = f32[32,32]{0,1:T(8,128)S(1)} all-reduce(f32[32,32]{0,1:T(8,128)S(1)} %fusion.57), channel_id=1, replica_groups=mesh['loop'=4,'inner'=8] {'loop','inner'}, use_global_device_ids=true, to_apply=%region_6.9 | all-reduce | flops 1024 | bytes 8192 | tf_op jit(solution)/shard_map/psum | solution.py:108
  159.9 39.5 %psum.37 = f32[32,32]{0,1:T(8,128)S(1)} all-reduce(f32[32,32]{0,1:T(8,128)S(1)} %fusion.58), channel_id=1, replica_groups=mesh['loop'=4,'inner'=8] {'loop','inner'}, use_global_device_ids=true, to_apply=%region_7.10 | all-reduce | flops 1024 | bytes 8192 | tf_op jit(solution)/shard_map/psum | solution.py:112
  199.4 2.9 cholesky.70
  203.7 2.4 custom-call.8
  207.7 4.8 %collective-permute-start.4 = (f32[256,32]{0,1:T(8,128)S(1)}, f32[256,32]{0,1:T(8,128)S(1)}, u32[]{:S(2)}, u32[]{:S(2)}) collective-permute-start(f32[256,32]{0,1:T(8,128)S(1)} %get-tuple-element.20), channel_id=1, source_target_pairs={{0,1},{1,2},{2,3},{3,4},{4,5},{5,6},{6,7},{8,9},{9,10},{10,11},{11... | collective-permute-start | bytes 98312 | tf_op jit(solution)/shard_map/ppermute | solution.py:18
  214.1 7.2 %all-gather.2 = f32[3072,32]{0,1:T(8,128)S(1)} all-gather(f32[768,32]{0,1:T(8,128)S(1)} %pad_maximum_fusion.2), channel_id=4, replica_groups=mesh['loop'=4,'inner'=8] {'loop'}, dimensions={0}, use_global_device_ids=true | all-gather | bytes 491520 | tf_op jit(solution)/shard_map/all_gather | solution.py:104
  221.3 2.8 convolution_multiply_fusion.2
  224.2 41.7 %psum.38 = f32[32,32]{0,1:T(8,128)S(1)} all-reduce(f32[32,32]{0,1:T(8,128)S(1)} %fusion.59), channel_id=1, replica_groups=mesh['loop'=4,'inner'=8] {'loop','inner'}, use_global_device_ids=true, to_apply=%region_8.11 | all-reduce | flops 1024 | bytes 8192 | tf_op jit(solution)/shard_map/psum | solution.py:108
  266.3 39.8 %psum.39 = f32[32,32]{0,1:T(8,128)S(1)} all-reduce(f32[32,32]{0,1:T(8,128)S(1)} %fusion.60), channel_id=1, replica_groups=mesh['loop'=4,'inner'=8] {'loop','inner'}, use_global_device_ids=true, to_apply=%region_9.12 | all-reduce | flops 1024 | bytes 8192 | tf_op jit(solution)/shard_map/psum | solution.py:112
  306.2 2.9 cholesky.81
  310.4 2.4 custom-call.9
  (64 shorter events, 16.2 us)
Async XLA Ops:
  7.2 31.2 %copy-start = (bf16[1024,32]{0,1:T(8,128)(2,1)S(1)}, bf16[1024,32]{0,1:T(8,128)(2,1)}, u32[]{:S(2)}) copy-start(bf16[1024,32]{0,1:T(8,128)(2,1)} %param.10) | copy-start | bytes 196612
  7.2 31.2 %copy-start.2 = (bf16[256,1024]{1,0:T(8,128)(2,1)S(1)}, bf16[256,1024]{1,0:T(8,128)(2,1)}, u32[]{:S(2)}) copy-start(bf16[256,1024]{1,0:T(8,128)(2,1)} %param.7) | copy-start | bytes 1572868
  7.2 31.0 %copy-start.3 = (s32[8192]{0:T(1024)S(1)}, s32[8192]{0:T(1024)}, u32[]{:S(2)}) copy-start(s32[8192]{0:T(1024)} %param.8) | copy-start | bytes 98308
  7.2 80.9 %copy-start.4 = (s32[256,2]{0,1:T(2,128)S(1)}, s32[256,2]{0,1:T(2,128)}, u32[]{:S(2)}) copy-start(s32[256,2]{0,1:T(2,128)} %param.9) | copy-start | bytes 6148
  7.2 81.4 %all-gather.5.cloned.1.call-start = ((), (), s32[]{:S(2)}) async-start(), calls=%async_computation | async-start | bytes 7864320 | tf_op jit(solution)/shard_map/all_gather | solution.py:54
  7.3 17.1 %collective-permute-start.1 = (bf16[256,1024]{1,0:T(8,128)(2,1)}, bf16[256,1024]{1,0:T(8,128)(2,1)S(1)}, u32[]{:S(2)}, u32[]{:S(2)}) collective-permute-start(bf16[256,1024]{1,0:T(8,128)(2,1)} %param.7), channel_id=1, source_target_pairs={{1,0},{2,1},{3,2},{4,3},{5,4},{6,5},{7,6},{9,8},{10,9},{11,10},{12... | collective-permute-start | bytes 1572872 | tf_op jit(solution)/shard_map/ppermute | solution.py:20
  8.7 27.2 %collective-permute-start = (bf16[256,1024]{1,0:T(8,128)(2,1)}, bf16[256,1024]{1,0:T(8,128)(2,1)S(1)}, u32[]{:S(2)}, u32[]{:S(2)}) collective-permute-start(bf16[256,1024]{1,0:T(8,128)(2,1)} %param.7), channel_id=1, source_target_pairs={{0,1},{1,2},{2,3},{3,4},{4,5},{5,6},{6,7},{8,9},{9,10},{10,11},{11... | collective-permute-start | bytes 1572872 | tf_op jit(solution)/shard_map/ppermute | solution.py:18
  88.7 4.6 %copy-start.1 = (bf16[3072,1024]{1,0:T(8,128)(2,1)S(1)}, bf16[3072,1024]{1,0:T(8,128)(2,1)}, u32[]{:S(2)}) copy-start(bf16[3072,1024]{1,0:T(8,128)(2,1)} %all-gather.5.cloned.1.call-done) | copy-start | bytes 18874372
  100.3 6.1 %collective-permute-start.3 = (f32[256,32]{0,1:T(8,128)S(1)}, f32[256,32]{0,1:T(8,128)S(1)}, u32[]{:S(2)}, u32[]{:S(2)}) collective-permute-start(f32[256,32]{0,1:T(8,128)S(1)} %get-tuple-element.18), channel_id=1, source_target_pairs={{1,0},{2,1},{3,2},{4,3},{5,4},{6,5},{7,6},{9,8},{10,9},{11,10},{12... | collective-permute-start | bytes 98312 | tf_op jit(solution)/shard_map/ppermute | solution.py:20
  101.6 6.4 %collective-permute-start.2 = (f32[256,32]{0,1:T(8,128)S(1)}, f32[256,32]{0,1:T(8,128)S(1)}, u32[]{:S(2)}, u32[]{:S(2)}) collective-permute-start(f32[256,32]{0,1:T(8,128)S(1)} %get-tuple-element.18), channel_id=1, source_target_pairs={{0,1},{1,2},{2,3},{3,4},{4,5},{5,6},{6,7},{8,9},{9,10},{10,11},{11... | collective-permute-start | bytes 98312 | tf_op jit(solution)/shard_map/ppermute | solution.py:18
  206.4 7.0 %collective-permute-start.5 = (f32[256,32]{0,1:T(8,128)S(1)}, f32[256,32]{0,1:T(8,128)S(1)}, u32[]{:S(2)}, u32[]{:S(2)}) collective-permute-start(f32[256,32]{0,1:T(8,128)S(1)} %get-tuple-element.20), channel_id=1, source_target_pairs={{1,0},{2,1},{3,2},{4,3},{5,4},{6,5},{7,6},{9,8},{10,9},{11,10},{12... | collective-permute-start | bytes 98312 | tf_op jit(solution)/shard_map/ppermute | solution.py:20
  207.7 6.4 %collective-permute-start.4 = (f32[256,32]{0,1:T(8,128)S(1)}, f32[256,32]{0,1:T(8,128)S(1)}, u32[]{:S(2)}, u32[]{:S(2)}) collective-permute-start(f32[256,32]{0,1:T(8,128)S(1)} %get-tuple-element.20), channel_id=1, source_target_pairs={{0,1},{1,2},{2,3},{3,4},{4,5},{5,6},{6,7},{8,9},{9,10},{10,11},{11... | collective-permute-start | bytes 98312 | tf_op jit(solution)/shard_map/ppermute | solution.py:18
Sparse Core Ops, SparseCore 0:
  38.3 48.3 all-gather.4
where the time goes:
time: 323 us; the launch traced here: 321 us
  blocking collectives  219 us (68%)
  other arithmetic  27.5 us (9%)
  waiting for transfers between devices  24 us (7%)
  starting transfers between devices  19.2 us (6%)
  matrix products  15.9 us (5%)
  between operations  14.4 us (4%)
    psum x2, blocking collectives, local(): projected = lax.psum(local_gram(current, image), ('loop', 'inner'))  83.1 us
    psum x2, blocking collectives, local(): gram_total = lax.psum(local_gram(image, image), ('loop', 'inner'))  79.3 us
    psum x1, blocking collectives, local(): lax.psum(local_gram(start_block, start_block), ('loop', 'inner'))  42.3 us
    ppermute x3, starting transfers between devices, extended(): lax.ppermute(tail, axis, [(i, (i + 1) % count) for i in range(ends)])  15.1 us
    all_gather x2, blocking collectives, local(): vec_strip = lax.all_gather(vec_side[None], 'loop', axis=0, tiled=True)  14.3 us
    ppermute x3, waiting for transfers between devices, extended(): lax.ppermute(tail, axis, [(i, (i + 1) % count) for i in range(ends)])  13.8 us
    another operation x9, other arithmetic, finish(): lower_factor = jnp.linalg.cholesky(gram_total)  10.8 us
    ppermute x3, waiting for transfers between devices, extended(): lax.ppermute(head, axis, [((i + 1) % count, i) for i in range(ends)])  10.2 us
  transfers between devices with their start and end apart: 7, of which 4 were waited for; matrix products, arithmetic and copies ran while one was open for 3% of the time, Pallas kernels for 0%

commit v1 on v0

--- a/solution.py
+++ b/solution.py
@@ -2,6 +2,7 @@
 import jax.numpy as jnp
 from jax import lax
 from jax.sharding import PartitionSpec as P
+from jax.lax import all_gather
 
 STEPS = 2
 BINS_COL = 8
@@ -92,7 +93,8 @@
     degree = jnp.sum(current_kernel(0), axis=1)
     inv_root = lax.rsqrt(degree)
     start_block = jnp.dot(snapshots, start_weights, preferred_element_type=jnp.float32)
-    start_total = lax.psum(local_gram(start_block, start_block), ("loop", "inner"))
+    panel = local_gram(start_block, start_block)
+    start_total = jnp.sum(all_gather(panel, axis_name=("loop", "inner")), axis=0)
     current, unused = finish(start_block, start_total)
     basis_blocks = [current]
     coefficients = []

time: 323 us -> 348 us (1.077)
  blocking collectives: 219 us -> 245 us
    all_gather x0 -> x1, blocking collectives: none -> 69.3 us  [local(): all_gather(panel, axis_name=('loop', 'inner'))]
    psum x1 -> x0, blocking collectives: 42.3 us -> none  [local(): lax.psum(local_gram(start_block, start_block), ('loop', 'inner'))]
where the time goes in v1:
time: 348 us; the launch traced here: 347 us
  blocking collectives  245 us (70%)
  other arithmetic  27.5 us (8%)
  waiting for transfers between devices  23.9 us (7%)
  starting transfers between devices  18.9 us (5%)
  matrix products  15.9 us (5%)
  between operations  14.4 us (4%)
    psum x2, blocking collectives, local(): projected = lax.psum(local_gram(current, image), ('loop', 'inner'))  82 us
    psum x2, blocking collectives, local(): gram_total = lax.psum(local_gram(image, image), ('loop', 'inner'))  79.4 us
    all_gather x1, blocking collectives, local(): all_gather(panel, axis_name=('loop', 'inner'))  69.3 us
    ppermute x3, starting transfers between devices, extended(): lax.ppermute(tail, axis, [(i, (i + 1) % count) for i in range(ends)])  14.9 us
    all_gather x2, blocking collectives, local(): vec_strip = lax.all_gather(vec_side[None], 'loop', axis=0, tiled=True)  13.9 us
    ppermute x3, waiting for transfers between devices, extended(): lax.ppermute(tail, axis, [(i, (i + 1) % count) for i in range(ends)])  13.8 us
    another operation x9, other arithmetic, finish(): lower_factor = jnp.linalg.cholesky(gram_total)  10.8 us
    ppermute x3, waiting for transfers between devices, extended(): lax.ppermute(head, axis, [((i + 1) % count, i) for i in range(ends)])  10.2 us
  transfers between devices with their start and end apart: 7, of which 4 were waited for; matrix products, arithmetic and copies ran while one was open for 3% of the time, Pallas kernels for 0%

profile of v1, /device:TPU:0, one launch (start us, length us, event | category | flops | bytes accessed | tf_op | source)
XLA Modules:
  0.0 346.6 jit_solution(15581234949017729407)
XLA Ops:
  8.7 5.5 %collective-permute-start = (bf16[256,1024]{1,0:T(8,128)(2,1)}, bf16[256,1024]{1,0:T(8,128)(2,1)S(1)}, u32[]{:S(2)}, u32[]{:S(2)}) collective-permute-start(bf16[256,1024]{1,0:T(8,128)(2,1)} %param.7), channel_id=1, source_target_pairs={{0,1},{1,2},{2,3},{3,4},{4,5},{5,6},{6,7},{8,9},{9,10},{10,11},{11... | collective-permute-start | bytes 1572872 | tf_op jit(solution)/shard_map/ppermute | solution.py:19
  14.2 10.2 %collective-permute-done.1 = bf16[256,1024]{1,0:T(8,128)(2,1)S(1)} collective-permute-done((bf16[256,1024]{1,0:T(8,128)(2,1)}, bf16[256,1024]{1,0:T(8,128)(2,1)S(1)}, u32[]{:S(2)}, u32[]{:S(2)}) %collective-permute-start.1) | collective-permute-done | bytes 524320 | tf_op jit(solution)/shard_map/ppermute | solution.py:21
  24.4 11.5 %collective-permute-done = bf16[256,1024]{1,0:T(8,128)(2,1)S(1)} collective-permute-done((bf16[256,1024]{1,0:T(8,128)(2,1)}, bf16[256,1024]{1,0:T(8,128)(2,1)S(1)}, u32[]{:S(2)}, u32[]{:S(2)}) %collective-permute-start) | collective-permute-done | bytes 524320 | tf_op jit(solution)/shard_map/ppermute | solution.py:19
  35.9 2.3 pad_maximum_fusion
  38.8 69.3 %all-gather = f32[1024,32]{1,0:T(8,128)S(1)} all-gather(f32[32,32]{1,0:T(8,128)S(1)} %fusion.56), channel_id=2, replica_groups=mesh['loop'=4,'inner'=8] {'loop','inner'}, dimensions={0}, use_global_device_ids=true | all-gather | bytes 135168 | tf_op jit(solution)/shard_map/all_gather | solution.py:97
  108.2 2.9 cholesky.59
  112.5 2.4 custom-call.7
  115.7 4.2 %multiply_reduce_fusion = f32[3072]{0:T(1024)S(1)} fusion(bf16[3072,1024]{1,0:T(8,128)(2,1)} %all-gather.6.cloned.1.call-done), kind=kLoop, calls=%fused_computation | loop fusion | flops 9434112 | bytes 6303744 | tf_op jit(solution)/shard_map/reduce_sum | solution.py:83
  120.3 4.0 %fusion.4 = f32[256,3072]{1,0:T(8,128)} fusion(bf16[3072,1024]{1,0:T(8,128)(2,1)S(1)} %copy-done.1, bf16[256,1024]{1,0:T(8,128)(2,1)S(1)} %copy-done.2, f32[3072]{0:T(1024)S(1)} %multiply_reduce_fusion, f32[256]{0:T(256)S(1)} %multiply_reduce_fusion.1), kind=kOutput, calls=%fused_computation.7 | convolution fusion | flops 1614544896 | bytes 9974784 | tf_op jit(solution)/shard_map/dot_general | solution.py:84
  124.3 2.8 fusion.52
  128.7 4.5 %collective-permute-start.2 = (f32[256,32]{0,1:T(8,128)S(1)}, f32[256,32]{0,1:T(8,128)S(1)}, u32[]{:S(2)}, u32[]{:S(2)}) collective-permute-start(f32[256,32]{0,1:T(8,128)S(1)} %get-tuple-element.20), channel_id=1, source_target_pairs={{0,1},{1,2},{2,3},{3,4},{4,5},{5,6},{6,7},{8,9},{9,10},{10,11},{11... | collective-permute-start | bytes 98312 | tf_op jit(solution)/shard_map/ppermute | solution.py:19
  134.8 6.7 %all-gather.2 = f32[3072,32]{0,1:T(8,128)S(1)} all-gather(f32[768,32]{0,1:T(8,128)S(1)} %pad_maximum_fusion.1), channel_id=4, replica_groups=mesh['loop'=4,'inner'=8] {'loop'}, dimensions={0}, use_global_device_ids=true | all-gather | bytes 491520 | tf_op jit(solution)/shard_map/all_gather | solution.py:106
  141.5 2.8 convolution_multiply_fusion.3
  144.5 40.4 %psum.28 = f32[32,32]{0,1:T(8,128)S(1)} all-reduce(f32[32,32]{0,1:T(8,128)S(1)} %fusion.57), channel_id=1, replica_groups=mesh['loop'=4,'inner'=8] {'loop','inner'}, use_global_device_ids=true, to_apply=%region_6.9 | all-reduce | flops 1024 | bytes 8192 | tf_op jit(solution)/shard_map/psum | solution.py:110
  185.2 39.8 %psum.29 = f32[32,32]{0,1:T(8,128)S(1)} all-reduce(f32[32,32]{0,1:T(8,128)S(1)} %fusion.58), channel_id=1, replica_groups=mesh['loop'=4,'inner'=8] {'loop','inner'}, use_global_device_ids=true, to_apply=%region_7.10 | all-reduce | flops 1024 | bytes 8192 | tf_op jit(solution)/shard_map/psum | solution.py:114
  225.1 2.9 cholesky.70
  229.3 2.4 custom-call.8
  233.3 4.8 %collective-permute-start.4 = (f32[256,32]{0,1:T(8,128)S(1)}, f32[256,32]{0,1:T(8,128)S(1)}, u32[]{:S(2)}, u32[]{:S(2)}) collective-permute-start(f32[256,32]{0,1:T(8,128)S(1)} %get-tuple-element.22), channel_id=1, source_target_pairs={{0,1},{1,2},{2,3},{3,4},{4,5},{5,6},{6,7},{8,9},{9,10},{10,11},{11... | collective-permute-start | bytes 98312 | tf_op jit(solution)/shard_map/ppermute | solution.py:19
  239.7 7.2 %all-gather.3 = f32[3072,32]{0,1:T(8,128)S(1)} all-gather(f32[768,32]{0,1:T(8,128)S(1)} %pad_maximum_fusion.2), channel_id=5, replica_groups=mesh['loop'=4,'inner'=8] {'loop'}, dimensions={0}, use_global_device_ids=true | all-gather | bytes 491520 | tf_op jit(solution)/shard_map/all_gather | solution.py:106
  246.9 2.8 convolution_multiply_fusion.2
  249.9 41.6 %psum.30 = f32[32,32]{0,1:T(8,128)S(1)} all-reduce(f32[32,32]{0,1:T(8,128)S(1)} %fusion.59), channel_id=1, replica_groups=mesh['loop'=4,'inner'=8] {'loop','inner'}, use_global_device_ids=true, to_apply=%region_8.11 | all-reduce | flops 1024 | bytes 8192 | tf_op jit(solution)/shard_map/psum | solution.py:110
  291.9 39.5 %psum.31 = f32[32,32]{0,1:T(8,128)S(1)} all-reduce(f32[32,32]{0,1:T(8,128)S(1)} %fusion.60), channel_id=1, replica_groups=mesh['loop'=4,'inner'=8] {'loop','inner'}, use_global_device_ids=true, to_apply=%region_9.12 | all-reduce | flops 1024 | bytes 8192 | tf_op jit(solution)/shard_map/psum | solution.py:114
  331.5 2.9 cholesky.81
  335.7 2.4 custom-call.9
  (65 shorter events, 16.2 us)
Async XLA Ops:
  7.2 31.2 %copy-start = (bf16[1024,32]{0,1:T(8,128)(2,1)S(1)}, bf16[1024,32]{0,1:T(8,128)(2,1)}, u32[]{:S(2)}) copy-start(bf16[1024,32]{0,1:T(8,128)(2,1)} %param.10) | copy-start | bytes 196612
  7.2 31.2 %copy-start.2 = (bf16[256,1024]{1,0:T(8,128)(2,1)S(1)}, bf16[256,1024]{1,0:T(8,128)(2,1)}, u32[]{:S(2)}) copy-start(bf16[256,1024]{1,0:T(8,128)(2,1)} %param.7) | copy-start | bytes 1572868
  7.2 31.0 %copy-start.3 = (s32[8192]{0:T(1024)S(1)}, s32[8192]{0:T(1024)}, u32[]{:S(2)}) copy-start(s32[8192]{0:T(1024)} %param.8) | copy-start | bytes 98308
  7.2 107.9 %copy-start.4 = (s32[256,2]{0,1:T(2,128)S(1)}, s32[256,2]{0,1:T(2,128)}, u32[]{:S(2)}) copy-start(s32[256,2]{0,1:T(2,128)} %param.9) | copy-start | bytes 6148
  7.2 108.5 %all-gather.6.cloned.1.call-start = ((), (), s32[]{:S(2)}) async-start(), calls=%async_computation | async-start | bytes 7864320 | tf_op jit(solution)/shard_map/all_gather | solution.py:55
  7.3 17.1 %collective-permute-start.1 = (bf16[256,1024]{1,0:T(8,128)(2,1)}, bf16[256,1024]{1,0:T(8,128)(2,1)S(1)}, u32[]{:S(2)}, u32[]{:S(2)}) collective-permute-start(bf16[256,1024]{1,0:T(8,128)(2,1)} %param.7), channel_id=1, source_target_pairs={{1,0},{2,1},{3,2},{4,3},{5,4},{6,5},{7,6},{9,8},{10,9},{11,10},{12... | collective-permute-start | bytes 1572872 | tf_op jit(solution)/shard_map/ppermute | solution.py:21
  8.7 27.2 %collective-permute-start = (bf16[256,1024]{1,0:T(8,128)(2,1)}, bf16[256,1024]{1,0:T(8,128)(2,1)S(1)}, u32[]{:S(2)}, u32[]{:S(2)}) collective-permute-start(bf16[256,1024]{1,0:T(8,128)(2,1)} %param.7), channel_id=1, source_target_pairs={{0,1},{1,2},{2,3},{3,4},{4,5},{5,6},{6,7},{8,9},{9,10},{10,11},{11... | collective-permute-start | bytes 1572872 | tf_op jit(solution)/shard_map/ppermute | solution.py:19
  115.7 4.6 %copy-start.1 = (bf16[3072,1024]{1,0:T(8,128)(2,1)S(1)}, bf16[3072,1024]{1,0:T(8,128)(2,1)}, u32[]{:S(2)}) copy-start(bf16[3072,1024]{1,0:T(8,128)(2,1)} %all-gather.6.cloned.1.call-done) | copy-start | bytes 18874372
  127.4 5.9 %collective-permute-start.3 = (f32[256,32]{0,1:T(8,128)S(1)}, f32[256,32]{0,1:T(8,128)S(1)}, u32[]{:S(2)}, u32[]{:S(2)}) collective-permute-start(f32[256,32]{0,1:T(8,128)S(1)} %get-tuple-element.20), channel_id=1, source_target_pairs={{1,0},{2,1},{3,2},{4,3},{5,4},{6,5},{7,6},{9,8},{10,9},{11,10},{12... | collective-permute-start | bytes 98312 | tf_op jit(solution)/shard_map/ppermute | solution.py:21
  128.7 6.1 %collective-permute-start.2 = (f32[256,32]{0,1:T(8,128)S(1)}, f32[256,32]{0,1:T(8,128)S(1)}, u32[]{:S(2)}, u32[]{:S(2)}) collective-permute-start(f32[256,32]{0,1:T(8,128)S(1)} %get-tuple-element.20), channel_id=1, source_target_pairs={{0,1},{1,2},{2,3},{3,4},{4,5},{5,6},{6,7},{8,9},{9,10},{10,11},{11... | collective-permute-start | bytes 98312 | tf_op jit(solution)/shard_map/ppermute | solution.py:19
  232.0 7.0 %collective-permute-start.5 = (f32[256,32]{0,1:T(8,128)S(1)}, f32[256,32]{0,1:T(8,128)S(1)}, u32[]{:S(2)}, u32[]{:S(2)}) collective-permute-start(f32[256,32]{0,1:T(8,128)S(1)} %get-tuple-element.22), channel_id=1, source_target_pairs={{1,0},{2,1},{3,2},{4,3},{5,4},{6,5},{7,6},{9,8},{10,9},{11,10},{12... | collective-permute-start | bytes 98312 | tf_op jit(solution)/shard_map/ppermute | solution.py:21
  233.3 6.4 %collective-permute-start.4 = (f32[256,32]{0,1:T(8,128)S(1)}, f32[256,32]{0,1:T(8,128)S(1)}, u32[]{:S(2)}, u32[]{:S(2)}) collective-permute-start(f32[256,32]{0,1:T(8,128)S(1)} %get-tuple-element.22), channel_id=1, source_target_pairs={{0,1},{1,2},{2,3},{3,4},{4,5},{5,6},{6,7},{8,9},{9,10},{10,11},{11... | collective-permute-start | bytes 98312 | tf_op jit(solution)/shard_map/ppermute | solution.py:19
Sparse Core Ops, SparseCore 0:
  38.3 48.8 all-gather.5
